TPU v7x, 32 devices: a whole 2x2x4 slice. The times are simulated.
32 devices in a mesh: dp: 8 (over z, y), mp: 4 (over x, core).
Axes of the slice: x: 2, y: 2, z: 4, core: 2. Of those that a mesh axis runs over, the one named last changes fastest.
Arguments:
- tokens: bfloat16 [32, 256, 1152], P('dp'), may hold values from -6 to 6
- condition: bfloat16 [32, 1152], P('dp'), may hold values from -6 to 6
- cotangent: bfloat16 [32, 256, 1152], P('dp'), may hold values from -12 to 12
- kept_index: int32 [32, 128], P('dp'), may hold values from 0 to 255, as said below
- skip_index: int32 [32, 128], P('dp'), may hold values from 0 to 255, as said below
- step_count: int32 [1], replicated, may hold values from 1 to 20
- ada_weight: float32 [1152, 6, 1152], P('dp', None, 'mp'), may hold values from -0.1875 to 0.1875
- qkv_weight: float32 [3, 1152, 1152], P(None, 'dp', 'mp'), may hold values from -0.1875 to 0.1875
- proj_weight: float32 [1152, 1152], P('mp', 'dp'), may hold values from -1 to 1
- fc1_weight: float32 [1152, 4608], P('dp', 'mp'), may hold values from -0.1875 to 0.1875
- fc2_weight: float32 [4608, 1152], P('mp', 'dp'), may hold values from -0.09375 to 0.09375
- ada_moment: float32 [1152, 6, 1152], P('dp', None, 'mp'), may hold values from -80 to 80
- qkv_moment: float32 [3, 1152, 1152], P(None, 'dp', 'mp'), may hold values from -80 to 80
- proj_moment: float32 [1152, 1152], P('mp', 'dp'), may hold values from -80 to 80
- fc1_moment: float32 [1152, 4608], P('dp', 'mp'), may hold values from -80 to 80
- fc2_moment: float32 [4608, 1152], P('mp', 'dp'), may hold values from -80 to 80
- ada_average: float32 [1152, 6, 1152], P('dp', None, 'mp'), may hold values from -0.1875 to 0.1875
- qkv_average: float32 [3, 1152, 1152], P(None, 'dp', 'mp'), may hold values from -0.1875 to 0.1875
- proj_average: float32 [1152, 1152], P('mp', 'dp'), may hold values from -1 to 1
- fc1_average: float32 [1152, 4608], P('dp', 'mp'), may hold values from -0.1875 to 0.1875
- fc2_average: float32 [4608, 1152], P('mp', 'dp'), may hold values from -0.09375 to 0.09375
Outputs:
- block_out: bfloat16 [32, 256, 1152], P('dp')
- tokens_grad: float32 [32, 256, 1152], P('dp')
- condition_grad: float32 [32, 1152], P('dp')
- ada_master: float32 [1152, 6, 1152], P('dp', None, 'mp')
- qkv_master: float32 [3, 1152, 1152], P(None, 'dp', 'mp')
- proj_master: float32 [1152, 1152], P('mp', 'dp')
- fc1_master: float32 [1152, 4608], P('dp', 'mp')
- fc2_master: float32 [4608, 1152], P('mp', 'dp')
- ada_momentum: float32 [1152, 6, 1152], P('dp', None, 'mp')
- qkv_momentum: float32 [3, 1152, 1152], P(None, 'dp', 'mp')
- proj_momentum: float32 [1152, 1152], P('mp', 'dp')
- fc1_momentum: float32 [1152, 4608], P('dp', 'mp')
- fc2_momentum: float32 [4608, 1152], P('mp', 'dp')
- ada_ema: float32 [1152, 6, 1152], P('dp', None, 'mp')
- qkv_ema: float32 [3, 1152, 1152], P(None, 'dp', 'mp')
- proj_ema: float32 [1152, 1152], P('mp', 'dp')
- fc1_ema: float32 [1152, 4608], P('dp', 'mp')
- fc2_ema: float32 [4608, 1152], P('mp', 'dp')
Inputs may be any that keep to these rules, and one draw needn't show every extreme that they name: `kept_index`: row b lists 128 distinct positions of image b in increasing order; row b of skip_index lists the other 128 positions in increasing order. `skip_index`: row b lists the positions of image b that kept_index does not, in increasing order.
All inputs are finite; a program needn't handle non-finite values.
Results may differ from a plain program's by a relative error of at most 0.012.
The roundings to bfloat16 on the way count: a program that leaves them out, or rounds other values in their place, can miss the bound.
Values may be sent and summed in bfloat16 or wider, within the bound.
No kernel may reach another device: no remote copies, remote signals or barrier semaphores. Data moves between devices by JAX's collectives and lax.ppermute only.
A program may use at most 192 MiB of HBM per device.

v0:
```python
from functools import partial
import math
import jax
import jax.numpy as jnp
from jax import lax
from jax.sharding import PartitionSpec as P

HEAD_DIM = 72
epsilon = 1e-06
momentum_rate = 0.9


def layer_norm(values):
    centered = values - jnp.mean(values, axis=-1, keepdims=True)
    inverse = lax.rsqrt(jnp.mean(centered * centered, axis=-1, keepdims=True) + epsilon)
    return (centered * inverse, inverse)


def norm_back(normed, inverse, gradient):
    return inverse * (
        gradient
        - jnp.mean(gradient, axis=-1, keepdims=True)
        - normed * jnp.mean(gradient * normed, axis=-1, keepdims=True)
    )


def pick_rows(values, index):
    return jnp.take_along_axis(values, index[:, :, None], axis=1)


def place_rows(kept_rows, other_rows, kept_index, skip_index):
    images = kept_index.shape[0]
    batch = jnp.arange(images, dtype=jnp.int32)[:, None]
    blank = jnp.zeros(
        (images, kept_index.shape[1] + skip_index.shape[1], kept_rows.shape[2]), kept_rows.dtype
    )
    return blank.at[batch, kept_index].set(kept_rows).at[batch, skip_index].set(other_rows)


def share_rows(values):
    return lax.psum_scatter(values, "mp", scatter_dimension=1, tiled=True)


def whole_rows(values):
    return lax.all_gather(values, "mp", axis=1, tiled=True)


def per_device(
    tokens,
    condition,
    cotangent,
    kept_index,
    skip_index,
    step_count,
    ada_weight,
    qkv_weight,
    proj_weight,
    fc1_weight,
    fc2_weight,
    ada_moment,
    qkv_moment,
    proj_moment,
    fc1_moment,
    fc2_moment,
    ada_average,
    qkv_average,
    proj_average,
    fc1_average,
    fc2_average,
):
    f32 = jnp.float32
    bf16 = jnp.bfloat16
    ada_low = ada_weight.astype(bf16)
    qkv_low = qkv_weight.astype(bf16)
    proj_low = proj_weight.astype(bf16)
    fc1_low = fc1_weight.astype(bf16)
    fc2_low = fc2_weight.astype(bf16)
    ada_full, qkv_full, proj_full, fc1_full, fc2_full = (
        lax.all_gather(ada_low, "dp", axis=0, tiled=True),
        lax.all_gather(qkv_low, "dp", axis=1, tiled=True),
        lax.all_gather(proj_low, "dp", axis=1, tiled=True),
        lax.all_gather(fc1_low, "dp", axis=0, tiled=True),
        lax.all_gather(fc2_low, "dp", axis=1, tiled=True),
    )
    images = tokens.shape[0]
    kept_count = kept_index.shape[1]
    local_width = qkv_full.shape[2]
    local_heads = local_width // HEAD_DIM
    score_scale = HEAD_DIM ** (-0.5)
    row_share = kept_count // lax.axis_size("mp")
    row_start = lax.axis_index("mp") * row_share

    def own_rows(values):
        return lax.dynamic_slice_in_dim(values, row_start, row_share, 1)

    cond_float = condition.astype(f32)
    silu_cond = jax.nn.silu(cond_float).astype(bf16)
    mod_part = jnp.einsum("bd,dkf->bkf", silu_cond, ada_full, preferred_element_type=f32)
    modulation = lax.all_gather(mod_part, "mp", axis=2, tiled=True)
    shift_one = modulation[:, 0, None, :]
    scale_one = modulation[:, 1, None, :]
    gate_one = modulation[:, 2, None, :]
    shift_two = modulation[:, 3, None, :]
    scale_two = modulation[:, 4, None, :]
    gate_two = modulation[:, 5, None, :]
    kept_rows = pick_rows(tokens, kept_index).astype(f32)
    normed_one, inverse_one = layer_norm(kept_rows)
    hidden = (normed_one * (1.0 + scale_one) + shift_one).astype(bf16)
    projected = jnp.einsum("bnd,tdf->tbnf", hidden, qkv_full, preferred_element_type=f32).astype(
        bf16
    )
    split_heads = projected.reshape(3, images, kept_count, local_heads, HEAD_DIM)
    query_heads = split_heads[0]
    key_heads = split_heads[1]
    value_heads = split_heads[2]
    scores = (
        jnp.einsum("bqhe,bkhe->bhqk", query_heads, key_heads, preferred_element_type=f32)
        * score_scale
    )
    row_max = jnp.max(scores, axis=-1, keepdims=True)
    exp_scores = jnp.exp(scores - row_max)
    row_total = jnp.sum(exp_scores, axis=-1, keepdims=True)
    log_total = row_max + jnp.log(row_total)
    probs = exp_scores / row_total
    attended = (
        jnp.einsum("bhqk,bkhe->bqhe", probs.astype(bf16), value_heads, preferred_element_type=f32)
        .astype(bf16)
        .reshape(images, kept_count, local_width)
    )
    attn_part = jnp.einsum("bnf,fd->bnd", attended, proj_full, preferred_element_type=f32)
    attn_out = share_rows(attn_part)
    residual = own_rows(kept_rows) + gate_one * attn_out
    normed_two, inverse_two = layer_norm(residual)
    hidden_two = whole_rows((normed_two * (1.0 + scale_two) + shift_two).astype(bf16))
    pre_act = jnp.einsum("bnd,df->bnf", hidden_two, fc1_full, preferred_element_type=f32)
    activated = jax.nn.gelu(pre_act, approximate=True).astype(bf16)
    mlp_part = jnp.einsum("bnf,fd->bnd", activated, fc2_full, preferred_element_type=f32)
    mlp_out = share_rows(mlp_part)
    kept_out = residual + gate_two * mlp_out
    kept_low = whole_rows(kept_out.astype(bf16))
    block_out = place_rows(kept_low, pick_rows(tokens, skip_index), kept_index, skip_index)
    ada_back, qkv_back, proj_back, fc1_back, fc2_back = (
        lax.all_gather(ada_low, "dp", axis=0, tiled=True),
        lax.all_gather(qkv_low, "dp", axis=1, tiled=True),
        lax.all_gather(proj_low, "dp", axis=1, tiled=True),
        lax.all_gather(fc1_low, "dp", axis=0, tiled=True),
        lax.all_gather(fc2_low, "dp", axis=1, tiled=True),
    )
    grad_float = cotangent.astype(f32)
    grad_kept = pick_rows(grad_float, kept_index)
    grad_here = own_rows(grad_kept)
    gate_two_grad = jnp.sum(grad_here * mlp_out, axis=1)
    mlp_out_grad = (gate_two * grad_kept).astype(bf16)
    fc2_grad = jnp.einsum("bnf,bnd->fd", activated, mlp_out_grad, preferred_element_type=f32)
    act_grad = jnp.einsum("bnd,fd->bnf", mlp_out_grad, fc2_back, preferred_element_type=f32)
    gelu_value, gelu_pull = jax.vjp(partial(jax.nn.gelu, approximate=True), pre_act)
    pre_grad = gelu_pull(act_grad)[0].astype(bf16)
    fc1_grad = jnp.einsum("bnd,bnf->df", hidden_two, pre_grad, preferred_element_type=f32)
    hidden_two_part = jnp.einsum("bnf,df->bnd", pre_grad, fc1_back, preferred_element_type=f32)
    hidden_two_grad = share_rows(hidden_two_part)
    shift_two_grad = jnp.sum(hidden_two_grad, axis=1)
    scale_two_grad = jnp.sum(hidden_two_grad * normed_two, axis=1)
    residual_grad = grad_here + norm_back(
        normed_two, inverse_two, hidden_two_grad * (1.0 + scale_two)
    )
    gate_one_grad = jnp.sum(residual_grad * attn_out, axis=1)
    attn_out_grad = whole_rows((gate_one * residual_grad).astype(bf16))
    proj_grad = jnp.einsum("bnf,bnd->fd", attended, attn_out_grad, preferred_element_type=f32)
    attended_grad = jnp.einsum(
        "bnd,fd->bnf", attn_out_grad, proj_back, preferred_element_type=f32
    ).astype(bf16)
    attended_grad = attended_grad.reshape(images, kept_count, local_heads, HEAD_DIM)
    again_scores = (
        jnp.einsum("bqhe,bkhe->bhqk", query_heads, key_heads, preferred_element_type=f32)
        * score_scale
    )
    again_probs = jnp.exp(again_scores - log_total)
    prob_grad = jnp.einsum(
        "bqhe,bkhe->bhqk", attended_grad, value_heads, preferred_element_type=f32
    )
    score_grad = (
        again_probs * (prob_grad - jnp.sum(prob_grad * again_probs, axis=-1, keepdims=True))
    ).astype(bf16)
    query_grad = (
        jnp.einsum("bhqk,bkhe->bqhe", score_grad, key_heads, preferred_element_type=f32)
        * score_scale
    )
    key_grad = (
        jnp.einsum("bhqk,bqhe->bkhe", score_grad, query_heads, preferred_element_type=f32)
        * score_scale
    )
    value_grad = jnp.einsum(
        "bhqk,bqhe->bkhe", again_probs.astype(bf16), attended_grad, preferred_element_type=f32
    )
    grad_rows = (
        jnp.stack([query_grad, key_grad, value_grad])
        .astype(bf16)
        .reshape(3, images, kept_count, local_width)
    )
    qkv_grad = jnp.einsum("tbnf,bnd->tdf", grad_rows, hidden, preferred_element_type=f32)
    hidden_part = jnp.einsum("tbnf,tdf->bnd", grad_rows, qkv_back, preferred_element_type=f32)
    hidden_grad = share_rows(hidden_part)
    normed_here = own_rows(normed_one)
    inverse_here = own_rows(inverse_one)
    shift_one_grad = jnp.sum(hidden_grad, axis=1)
    scale_one_grad = jnp.sum(hidden_grad * normed_here, axis=1)
    kept_share = residual_grad + norm_back(
        normed_here, inverse_here, hidden_grad * (1.0 + scale_one)
    )
    kept_grad = lax.all_gather(kept_share, "mp", axis=1, tiled=True)
    tokens_grad = place_rows(kept_grad, pick_rows(grad_float, skip_index), kept_index, skip_index)
    mod_grad = jnp.stack(
        [
            shift_one_grad,
            scale_one_grad,
            gate_one_grad,
            shift_two_grad,
            scale_two_grad,
            gate_two_grad,
        ],
        axis=1,
    )
    mod_local = lax.psum_scatter(mod_grad, "mp", scatter_dimension=2, tiled=True).astype(bf16)
    ada_grad = jnp.einsum("bd,bkf->dkf", silu_cond, mod_local, preferred_element_type=f32)
    silu_grad = lax.psum(
        jnp.einsum("bkf,dkf->bd", mod_local, ada_back, preferred_element_type=f32), "mp"
    )
    silu_value, silu_pull = jax.vjp(jax.nn.silu, cond_float)
    condition_grad = silu_pull(silu_grad)[0]
    ada_shard, qkv_shard, proj_shard, fc1_shard, fc2_shard = (
        lax.psum_scatter(ada_grad, "dp", scatter_dimension=0, tiled=True),
        lax.psum_scatter(qkv_grad, "dp", scatter_dimension=1, tiled=True),
        lax.psum_scatter(proj_grad, "dp", scatter_dimension=1, tiled=True),
        lax.psum_scatter(fc1_grad, "dp", scatter_dimension=0, tiled=True),
        lax.psum_scatter(fc2_grad, "dp", scatter_dimension=1, tiled=True),
    )
    rate = 0.02 / math.sqrt(images * lax.axis_size("dp") * kept_count)
    step_float = step_count.astype(f32)[0]
    decay = (1.0 + step_float) / (10.0 + step_float)

    def update(weight, moment, average, gradient):
        new_moment = momentum_rate * moment + gradient
        master = weight - rate * (gradient + momentum_rate * new_moment)
        return (master, new_moment, decay * average + (1.0 - decay) * master)

    ada_master, ada_momentum, ada_ema = update(ada_weight, ada_moment, ada_average, ada_shard)
    qkv_master, qkv_momentum, qkv_ema = update(qkv_weight, qkv_moment, qkv_average, qkv_shard)
    proj_master, proj_momentum, proj_ema = update(
        proj_weight, proj_moment, proj_average, proj_shard
    )
    fc1_master, fc1_momentum, fc1_ema = update(fc1_weight, fc1_moment, fc1_average, fc1_shard)
    fc2_master, fc2_momentum, fc2_ema = update(fc2_weight, fc2_moment, fc2_average, fc2_shard)
    return (
        block_out,
        tokens_grad,
        condition_grad,
        ada_master,
        qkv_master,
        proj_master,
        fc1_master,
        fc2_master,
        ada_momentum,
        qkv_momentum,
        proj_momentum,
        fc1_momentum,
        fc2_momentum,
        ada_ema,
        qkv_ema,
        proj_ema,
        fc1_ema,
        fc2_ema,
    )


def solution(mesh):
    placed = (
        P("dp", None, None),
        P("dp", None),
        P("dp", None, None),
        P("dp", None),
        P("dp", None),
        P(),
        P("dp", None, "mp"),
        P(None, "dp", "mp"),
        P("mp", "dp"),
        P("dp", "mp"),
        P("mp", "dp"),
        P("dp", None, "mp"),
        P(None, "dp", "mp"),
        P("mp", "dp"),
        P("dp", "mp"),
        P("mp", "dp"),
        P("dp", None, "mp"),
        P(None, "dp", "mp"),
        P("mp", "dp"),
        P("dp", "mp"),
        P("mp", "dp"),
    )
    return jax.shard_map(
        per_device,
        mesh=mesh,
        in_specs=placed,
        out_specs=(
            P("dp", None, None),
            P("dp", None, None),
            P("dp", None),
            P("dp", None, "mp"),
            P(None, "dp", "mp"),
            P("mp", "dp"),
            P("dp", "mp"),
            P("mp", "dp"),
            P("dp", None, "mp"),
            P(None, "dp", "mp"),
            P("mp", "dp"),
            P("dp", "mp"),
            P("mp", "dp"),
            P("dp", None, "mp"),
            P(None, "dp", "mp"),
            P("mp", "dp"),
            P("dp", "mp"),
            P("mp", "dp"),
        ),
        check_vma=False,
    )
```

profile of v0, /device:TPU:0, one launch (start us, length us, event | category | flops | bytes accessed | tf_op | source)
XLA Modules:
  0.0 1142.5 jit_solution(12994166128726137092)
XLA Ops:
  11.3 5.7 gather_fusion
  18.1 38.6 %all_gather.38 = bf16[288,1152]{0,1:T(8,128)(2,1)} all-gather(bf16[288,144]{0,1:T(8,128)(2,1)S(1)} %copy-done.21), channel_id=1, replica_groups=mesh['dp'=8,'mp'=4] {'dp'}, dimensions={1}, use_global_device_ids=true | all-gather | bytes 746496 | tf_op jit(solution)/shard_map/all_gather | solution.py:81
  56.7 51.9 %all-gather.9.cloned.1.call-done = bf16[1152,6,288]{2,0,1:T(8,128)(2,1)} async-done(((bf16[144,6,288]{2,0,1:T(8,128)(2,1)}), bf16[1152,6,288]{2,0,1:T(8,128)(2,1)}) %all-gather.9.cloned.1.call-update) | async-done | bytes 3981328 | tf_op jit(solution)/shard_map/all_gather | solution.py:79
  114.4 17.3 %all_gather.36 = f32[4,6,1152]{1,0,2:T(4,128)S(1)} all-gather(f32[4,6,288]{1,0,2:T(4,128)} %copy.115), channel_id=1, replica_groups=mesh['dp'=8,'mp'=4] {'mp'}, dimensions={2}, use_global_device_ids=true | all-gather | bytes 138240 | tf_op jit(solution)/shard_map/all_gather | solution.py:99
  131.7 9.2 fusion.74
  147.7 17.1 %all-gather.11.cloned.1.call-done = bf16[3,1152,288]{2,1,0:T(8,128)(2,1)} async-done(((bf16[3,144,288]{2,1,0:T(8,128)(2,1)}), bf16[3,1152,288]{2,1,0:T(8,128)(2,1)}) %all-gather.11.cloned.1.call-update) | async-done | bytes 1990672 | tf_op jit(solution)/shard_map/all_gather | solution.py:80
  186.2 18.3 %reduce-scatter.15.cloned.1.call-done = f32[4,32,1152]{2,1,0:T(8,128)} async-done(((f32[4,128,1152]{2,1,0:T(8,128)}), f32[4,32,1152]{2,1,0:T(8,128)}) %reduce-scatter.15.cloned.1.call-update) | async-done | bytes 589840 | tf_op jit(solution)/shard_map/reduce_scatter | solution.py:41
  212.0 11.0 gather_fusion.2
  230.0 32.5 %all-gather.15.cloned.1.call-done = bf16[1152,1152]{1,0:T(8,128)(2,1)} async-done(((bf16[144,1152]{1,0:T(8,128)(2,1)}), bf16[1152,1152]{1,0:T(8,128)(2,1)}) %all-gather.15.cloned.1.call-update) | async-done | bytes 2654224 | tf_op jit(solution)/shard_map/all_gather | solution.py:82
  262.5 18.1 %all-gather.13.cloned.1.call-done = bf16[4,128,1152]{2,1,0:T(8,128)(2,1)} async-done(((bf16[4,32,1152]{2,1,0:T(8,128)(2,1)}), bf16[4,128,1152]{2,1,0:T(8,128)(2,1)}) %all-gather.13.cloned.1.call-update) | async-done | bytes 1179664 | tf_op jit(solution)/shard_map/all_gather | solution.py:45
  291.1 103.6 %reduce-scatter.29.cloned.1.call-done = f32[1152,144]{0,1:T(8,128)} async-done(((f32[1152,1152]{0,1:T(8,128)}), f32[1152,144]{0,1:T(8,128)}) %reduce-scatter.29.cloned.1.call-update) | async-done | bytes 663568 | tf_op jit(solution)/shard_map/reduce_scatter | solution.py:235
  398.2 54.9 %all-gather.17.cloned.1.call-done = bf16[1152,1152]{0,1:T(8,128)(2,1)} async-done(((bf16[1152,144]{0,1:T(8,128)(2,1)}), bf16[1152,1152]{0,1:T(8,128)(2,1)}) %all-gather.17.cloned.1.call-update) | async-done | bytes 2654224 | tf_op jit(solution)/shard_map/all_gather | solution.py:83
  453.1 5.8 fusion.17
  463.6 6.1 fusion.2
  469.7 25.4 %reduce-scatter.19.cloned.1.call-done = f32[4,32,1152]{2,1,0:T(8,128)} async-done(((f32[4,128,1152]{2,1,0:T(8,128)}), f32[4,32,1152]{2,1,0:T(8,128)}) %reduce-scatter.19.cloned.1.call-update) | async-done | bytes 589840 | tf_op jit(solution)/shard_map/reduce_scatter | solution.py:41
  497.9 33.0 %reduce-scatter.17.cloned.1.call-done = f32[4,32,1152]{2,1,0:T(8,128)} async-done(((f32[4,128,1152]{2,1,0:T(8,128)}), f32[4,32,1152]{2,1,0:T(8,128)}) %reduce-scatter.17.cloned.1.call-update) | async-done | bytes 589840 | tf_op jit(solution)/shard_map/reduce_scatter | solution.py:41
  536.8 16.8 %all-gather.21.cloned.1.call-done = bf16[4,128,1152]{2,1,0:T(8,128)(2,1)} async-done(((bf16[4,32,1152]{2,1,0:T(8,128)(2,1)}), bf16[4,128,1152]{2,1,0:T(8,128)(2,1)}) %all-gather.21.cloned.1.call-update) | async-done | bytes 1179664 | tf_op jit(solution)/shard_map/all_gather | solution.py:45
  562.4 33.2 %reduce-scatter.21.cloned.1.call-done = f32[4,32,1152]{2,1,0:T(8,128)} async-done(((f32[4,128,1152]{2,1,0:T(8,128)}), f32[4,32,1152]{2,1,0:T(8,128)}) %reduce-scatter.21.cloned.1.call-update) | async-done | bytes 589840 | tf_op jit(solution)/shard_map/reduce_scatter | solution.py:41
  616.5 5.8 convolution_bitcast_fusion.1
  627.6 8.6 copy.147
  636.2 9.0 reshape.214
  651.3 5.7 fusion.46
  658.4 11.0 gather_fusion.3
  669.4 8.4 gather_fusion.1
  688.4 78.5 %scatter_fusion = bf16[4,256,1152]{2,1,0:T(8,128)(2,1)} fusion(bf16[4,256,1152]{2,1,0:T(8,128)(2,1)} %broadcast_in_dim.28, s32[512]{0:T(512)S(1)} %get-tuple-element.152, bf16[512,1152]{1,0:T(8,128)(2,1)} %bitcast.198), kind=kCustom, calls=%fused_computation.4 | custom fusion | bytes 3543040 | tf_op jit(solution)/shard_map/scatter | solution.py:37
  766.9 78.8 %scatter_fusion.1 = bf16[4,256,1152]{2,1,0:T(8,128)(2,1)} fusion(bf16[4,256,1152]{2,1,0:T(8,128)(2,1)} %scatter_fusion, s32[512]{0:T(512)S(1)} %get-tuple-element.150, bf16[512,1152]{1,0:T(8,128)(2,1)} %bitcast.187), kind=kCustom, calls=%fused_computation.5 | custom fusion | bytes 3543040 | tf_op jit(solution)/shard_map/scatter | solution.py:37
  854.9 11.2 psum.7
  866.8 55.1 %reduce-scatter.33.cloned.1.call-done = f32[144,864]{1,0:T(8,128)} async-done(((f32[1152,864]{1,0:T(8,128)}), f32[144,864]{1,0:T(8,128)}) %reduce-scatter.33.cloned.1.call-update) | async-done | bytes 497680
  936.3 10.9 all-gather.23.cloned.1.call-done
  949.7 80.0 %scatter_fusion.2 = f32[4,256,1152]{2,1,0:T(8,128)} fusion(f32[4,256,1152]{2,1,0:T(8,128)} %broadcast_in_dim.35, s32[512]{0:T(512)S(1)} %get-tuple-element.152, f32[512,1152]{1,0:T(8,128)} %bitcast.196), kind=kCustom, calls=%fused_computation.6 | custom fusion | bytes 7081984 | tf_op jit(solution)/shard_map/scatter | solution.py:37
  1029.7 79.8 %scatter_fusion.3 = f32[4,256,1152]{2,1,0:T(8,128)} fusion(f32[4,256,1152]{2,1,0:T(8,128)} %scatter_fusion.2, s32[512]{0:T(512)S(1)} %get-tuple-element.150, f32[512,1152]{1,0:T(8,128)} %bitcast.184), kind=kCustom, calls=%fused_computation.7 | custom fusion | bytes 7081984 | tf_op jit(solution)/shard_map/scatter | solution.py:37
  1109.5 21.1 %reduce-scatter.23.cloned.1.call-done = f32[144,6,288]{2,0,1:T(8,128)} async-done(((f32[1152,6,288]{2,0,1:T(8,128)}), f32[144,6,288]{2,0,1:T(8,128)}) %reduce-scatter.23.cloned.1.call-update) | async-done | bytes 995344 | tf_op jit(solution)/shard_map/reduce_scatter | solution.py:231
  (217 shorter events, 164.5 us)
Async XLA Ops:
  7.2 4.1 copy-start
  7.2 2.5 copy-start.14
  7.2 3.4 copy-start.19
  7.2 4.0 copy-start.39
  7.2 101.4 %all-gather.9.cloned.1.call-start = ((), (), s32[]{:S(2)}) async-start(), calls=%async_computation.10 | async-start | bytes 5971968 | tf_op jit(solution)/shard_map/all_gather | solution.py:79
  9.7 155.0 %all-gather.11.cloned.1.call-start = ((), (), s32[]{:S(2)}) async-start(), calls=%async_computation.11 | async-start | bytes 2985984 | tf_op jit(solution)/shard_map/all_gather | solution.py:80
  10.5 194.0 %reduce-scatter.15.cloned.1.call-start = ((), (), s32[]{:S(2)}) async-start(), calls=%async_computation.12 | async-start | bytes 2949120 | tf_op jit(solution)/shard_map/reduce_scatter | solution.py:41
  17.5 147.2 %copy-start.32 = (f32[4,128]{1,0:T(4,128)}, f32[4,128]{1,0:T(4,128)S(1)}, u32[]{:S(2)}) copy-start(f32[4,128]{1,0:T(4,128)S(1)} %broadcast_multiply_fusion.5) | copy-start | bytes 6148
  18.1 146.7 %copy-start.34 = (f32[4,128]{1,0:T(4,128)}, f32[4,128]{1,0:T(4,128)S(1)}, u32[]{:S(2)}) copy-start(f32[4,128]{1,0:T(4,128)S(1)} %add_rsqrt_fusion.1) | copy-start | bytes 6148
  172.8 89.7 %all-gather.15.cloned.1.call-start = ((), (), s32[]{:S(2)}) async-start(), calls=%async_computation.14 | async-start | bytes 2985984 | tf_op jit(solution)/shard_map/all_gather | solution.py:82
  174.7 105.9 %all-gather.13.cloned.1.call-start = ((), (), s32[]{:S(2)}) async-start(), calls=%async_computation.13 | async-start | bytes 1474560 | tf_op jit(solution)/shard_map/all_gather | solution.py:45
  207.8 186.9 %reduce-scatter.29.cloned.1.call-start = ((), (), s32[]{:S(2)}) async-start(), calls=%async_computation.25 | async-start | bytes 5971968 | tf_op jit(solution)/shard_map/reduce_scatter | solution.py:235
  280.6 5.5 copy-start.8
  280.6 5.5 copy-start.29
  290.4 162.7 %all-gather.17.cloned.1.call-start = ((), (), s32[]{:S(2)}) async-start(), calls=%async_computation.15 | async-start | bytes 2985984 | tf_op jit(solution)/shard_map/all_gather | solution.py:83
  398.2 97.0 %reduce-scatter.19.cloned.1.call-start = ((), (), s32[]{:S(2)}) async-start(), calls=%async_computation.18 | async-start | bytes 2949120 | tf_op jit(solution)/shard_map/reduce_scatter | solution.py:41
  453.1 6.8 copy-start.42
  463.3 67.6 %reduce-scatter.17.cloned.1.call-start = ((), (), s32[]{:S(2)}) async-start(), calls=%async_computation.16 | async-start | bytes 2949120 | tf_op jit(solution)/shard_map/reduce_scatter | solution.py:41
  469.7 83.9 %all-gather.21.cloned.1.call-start = ((), (), s32[]{:S(2)}) async-start(), calls=%async_computation.19 | async-start | bytes 1474560 | tf_op jit(solution)/shard_map/all_gather | solution.py:45
  530.9 4.3 copy-start.26
  536.0 59.6 %reduce-scatter.21.cloned.1.call-start = ((), (), s32[]{:S(2)}) async-start(), calls=%async_computation.20 | async-start | bytes 2949120 | tf_op jit(solution)/shard_map/reduce_scatter | solution.py:41
  562.4 87.2 %reduce-scatter.31.cloned.1.call-start = ((), (), s32[]{:S(2)}) async-start(), calls=%async_computation.26 | async-start | bytes 737280
  612.2 74.7 %all-gather.19.cloned.1.call-start = ((), (), s32[]{:S(2)}) async-start(), calls=%async_computation.17 | async-start | bytes 1474560 | tf_op jit(solution)/shard_map/all_gather | solution.py:45
  612.9 232.7 %reduce-scatter.25.cloned.1.call-start = ((), (), s32[]{:S(2)}) async-start(), calls=%async_computation.23 | async-start | bytes 1990656 | tf_op jit(solution)/shard_map/reduce_scatter | solution.py:233
  616.4 231.3 %reduce-scatter.27.cloned.1.call-start = ((), (), s32[]{:S(2)}) async-start(), calls=%async_computation.24 | async-start | bytes 5971968 | tf_op jit(solution)/shard_map/reduce_scatter | solution.py:234
  622.3 299.6 %reduce-scatter.33.cloned.1.call-start = ((), (), s32[]{:S(2)}) async-start(), calls=%async_computation.27 | async-start | bytes 4644864
  645.2 6.0 copy-start.27
  645.2 302.0 %all-gather.23.cloned.1.call-start = ((), (), s32[]{:S(2)}) async-start(), calls=%async_computation.21 | async-start | bytes 2949120 | tf_op jit(solution)/shard_map/all_gather | solution.py:210
  649.6 481.1 %reduce-scatter.23.cloned.1.call-start = ((), (), s32[]{:S(2)}) async-start(), calls=%async_computation.22 | async-start | bytes 11943936 | tf_op jit(solution)/shard_map/reduce_scatter | solution.py:231
  682.5 2.7 copy-start.4
  766.9 78.8 %copy-start.20 = (f32[288,144]{0,1:T(8,128)S(1)}, f32[288,144]{0,1:T(8,128)}, u32[]{:S(2)}) copy-start(f32[288,144]{0,1:T(8,128)} %param.33) | copy-start | bytes 497668
  930.2 4.9 copy-start.9
  (31 other events, 38.8 us)
Sparse Core Ops, SparseCore 0:
  10.9 97.7 all-gather.8
  111.5 53.2 all-gather.10
  172.9 31.5 reduce-scatter.14
  207.4 55.0 all-gather.14
  264.5 16.0 all-gather.12
  290.5 104.1 reduce-scatter.28
  398.3 54.7 all-gather.16
  463.4 31.6 reduce-scatter.18
  497.8 33.0 reduce-scatter.16
  536.1 17.4 all-gather.20
  562.5 33.0 reduce-scatter.20
  612.3 22.0 reduce-scatter.30
  636.6 17.4 all-gather.18
  657.8 66.3 reduce-scatter.24
  727.6 102.9 reduce-scatter.26
  834.5 87.4 reduce-scatter.32
  923.3 23.8 all-gather.22
  950.6 179.9 reduce-scatter.22
where the time goes:
time: 1160 us; the launch traced here: 1140 us
  waiting for transfers between devices  493 us (42%)
  local copies, waits for them, and re-layouts  442 us (38%)
  blocking collectives  67.2 us (6%)
  matrix products  65 us (6%)
  other arithmetic  57.6 us (5%)
  between operations  15.7 us (1%)
    scatter x4, local copies, waits for them, and re-layouts, place_rows(): blank.at[batch, kept_index].set(kept_rows).at[batch, skip_index]  317 us
    reduce_scatter x4, waiting for transfers between devices, share_rows(): return lax.psum_scatter(values, 'mp', scatter_dimension=1, tiled=True)  110 us
    reduce_scatter x1, waiting for transfers between devices, per_device(): lax.psum_scatter(fc2_grad, 'dp', scatter_dimension=1, tiled=True)  104 us
    unnamed x111, local copies, waits for them, and re-layouts  61.3 us
    unnamed x20, waiting for transfers between devices  56.1 us
    all_gather x1, waiting for transfers between devices, per_device(): lax.all_gather(fc2_low, 'dp', axis=1, tiled=True)  54.9 us
    all_gather x1, waiting for transfers between devices, per_device(): lax.all_gather(ada_low, 'dp', axis=0, tiled=True)  51.9 us
    all_gather x1, blocking collectives, per_device(): lax.all_gather(proj_low, 'dp', axis=1, tiled=True)  38.6 us
  transfers between devices with their start and end apart: 18, of which 14 were waited for; matrix products, arithmetic and copies ran while one was open for 43% of the time, Pallas kernels for 0%

commit v1 on v0

--- a/solution.py
+++ b/solution.py
@@ -10,6 +10,23 @@
 momentum_rate = 0.9
 
 
+def fix_paths(x_part):
+    axis_id = "mp"
+    item_now = jax.lax.axis_size(axis_id)
+    plain = jax.lax.axis_index(axis_id)
+    z1, block_next, all_values = (item_now, plain, x_part.shape[1])
+    shaped, main = (x_part, 1)
+    while main < z1:
+        queue = []
+        for tick in range(z1):
+            queue.append((tick, (tick - main) % z1))
+        shaped = jnp.concatenate(
+            [shaped, jax.lax.ppermute(shaped, axis_name=axis_id, perm=queue)], 1
+        )
+        main = 2 * main
+    return jnp.roll(shaped, block_next * all_values, 1)
+
+
 def layer_norm(values):
     centered = values - jnp.mean(values, axis=-1, keepdims=True)
     inverse = lax.rsqrt(jnp.mean(centered * centered, axis=-1, keepdims=True) + epsilon)
@@ -42,7 +59,7 @@
 
 
 def whole_rows(values):
-    return lax.all_gather(values, "mp", axis=1, tiled=True)
+    return fix_paths(values)
 
 
 def per_device(

time: 1160 us -> 1130 us (0.974)
  waiting for transfers between devices: 493 us -> 441 us
  other arithmetic: 57.6 us -> 69.6 us
    all_gather x3 -> x0, waiting for transfers between devices: 35 us -> none  [whole_rows(): return lax.all_gather(values, 'mp', axis=1, tiled=True)]
    unnamed x20 -> x17, waiting for transfers between devices: 56.1 us -> 28.1 us
    ppermute x0 -> x6, waiting for transfers between devices: none -> 25.8 us  [fix_paths(): jax.lax.ppermute(shaped, axis_name=axis_id, perm=queue)]
    all_gather x1, waiting for transfers between devices: 32.5 us -> 18.1 us  [per_device(): lax.all_gather(fc1_low, 'dp', axis=0, tiled=True)]
    unnamed x111 -> x121, local copies, waits for them, and re-layouts: 61.3 us -> 61.6 us
  transfers between devices with their start and end apart: 18 -> 21, of which waited for: 14 -> 15; matrix products, arithmetic and copies ran while one was open for 43% -> 46% of each run, Pallas kernels for 0% -> 0%
where the time goes in v1:
time: 1130 us; the launch traced here: 1110 us
  local copies, waits for them, and re-layouts  443 us (39%)
  waiting for transfers between devices  441 us (39%)
  other arithmetic  69.6 us (6%)
  blocking collectives  67.3 us (6%)
  matrix products  63.3 us (6%)
  between operations  15.7 us (1%)
    scatter x4, local copies, waits for them, and re-layouts, place_rows(): blank.at[batch, kept_index].set(kept_rows).at[batch, skip_index]  317 us
    reduce_scatter x4, waiting for transfers between devices, share_rows(): return lax.psum_scatter(values, 'mp', scatter_dimension=1, tiled=True)  111 us
    reduce_scatter x1, waiting for transfers between devices, per_device(): lax.psum_scatter(fc2_grad, 'dp', scatter_dimension=1, tiled=True)  102 us
    unnamed x121, local copies, waits for them, and re-layouts  61.6 us
    all_gather x1, waiting for transfers between devices, per_device(): lax.all_gather(fc2_low, 'dp', axis=1, tiled=True)  54.5 us
    all_gather x1, waiting for transfers between devices, per_device(): lax.all_gather(ada_low, 'dp', axis=0, tiled=True)  52 us
    all_gather x1, blocking collectives, per_device(): lax.all_gather(proj_low, 'dp', axis=1, tiled=True)  38.6 us
    gather x4, local copies, waits for them, and re-layouts, pick_rows(): return jnp.take_along_axis(values, index[:, :, None], axis=1)  36 us
  transfers between devices with their start and end apart: 21, of which 15 were waited for; matrix products, arithmetic and copies ran while one was open for 46% of the time, Pallas kernels for 0%

profile of v1, /device:TPU:0, one launch (start us, length us, event | category | flops | bytes accessed | tf_op | source)
XLA Modules:
  0.0 1105.6 jit_solution(14315916173391728677)
XLA Ops:
  11.3 5.7 gather_fusion
  18.1 38.6 %all_gather.29 = bf16[288,1152]{0,1:T(8,128)(2,1)} all-gather(bf16[288,144]{0,1:T(8,128)(2,1)S(1)} %copy-done.24), channel_id=1, replica_groups=mesh['dp'=8,'mp'=4] {'dp'}, dimensions={1}, use_global_device_ids=true | all-gather | bytes 746496 | tf_op jit(solution)/shard_map/all_gather | solution.py:98
  56.7 52.0 %all-gather.6.cloned.1.call-done = bf16[1152,6,288]{2,0,1:T(8,128)(2,1)} async-done(((bf16[144,6,288]{2,0,1:T(8,128)(2,1)}), bf16[1152,6,288]{2,0,1:T(8,128)(2,1)}) %all-gather.6.cloned.1.call-update) | async-done | bytes 3981328 | tf_op jit(solution)/shard_map/all_gather | solution.py:96
  114.4 17.3 %all_gather.27 = f32[4,6,1152]{1,0,2:T(4,128)S(1)} all-gather(f32[4,6,288]{1,0,2:T(4,128)} %copy.123), channel_id=1, replica_groups=mesh['dp'=8,'mp'=4] {'mp'}, dimensions={2}, use_global_device_ids=true | all-gather | bytes 138240 | tf_op jit(solution)/shard_map/all_gather | solution.py:116
  131.8 9.1 fusion.89
  147.7 17.1 %all-gather.8.cloned.1.call-done = bf16[3,1152,288]{2,1,0:T(8,128)(2,1)} async-done(((bf16[3,144,288]{2,1,0:T(8,128)(2,1)}), bf16[3,1152,288]{2,1,0:T(8,128)(2,1)}) %all-gather.8.cloned.1.call-update) | async-done | bytes 1990672 | tf_op jit(solution)/shard_map/all_gather | solution.py:97
  186.8 17.8 %reduce-scatter.15.cloned.1.call-done = f32[4,32,1152]{2,1,0:T(8,128)} async-done(((f32[4,128,1152]{2,1,0:T(8,128)}), f32[4,32,1152]{2,1,0:T(8,128)}) %reduce-scatter.15.cloned.1.call-update) | async-done | bytes 589840 | tf_op jit(solution)/shard_map/reduce_scatter | solution.py:58
  211.9 11.0 gather_fusion.2
  233.3 7.6 collective-permute-done.1
  244.4 18.1 %all-gather.10.cloned.1.call-done = bf16[1152,1152]{1,0:T(8,128)(2,1)} async-done(((bf16[144,1152]{1,0:T(8,128)(2,1)}), bf16[1152,1152]{1,0:T(8,128)(2,1)}) %all-gather.10.cloned.1.call-update) | async-done | bytes 2654224 | tf_op jit(solution)/shard_map/all_gather | solution.py:99
  273.0 102.2 %reduce-scatter.29.cloned.1.call-done = f32[1152,144]{0,1:T(8,128)} async-done(((f32[1152,1152]{0,1:T(8,128)}), f32[1152,144]{0,1:T(8,128)}) %reduce-scatter.29.cloned.1.call-update) | async-done | bytes 663568 | tf_op jit(solution)/shard_map/reduce_scatter | solution.py:252
  379.1 54.5 %all-gather.12.cloned.1.call-done = bf16[1152,1152]{0,1:T(8,128)(2,1)} async-done(((bf16[1152,144]{0,1:T(8,128)(2,1)}), bf16[1152,1152]{0,1:T(8,128)(2,1)}) %all-gather.12.cloned.1.call-update) | async-done | bytes 2654224 | tf_op jit(solution)/shard_map/all_gather | solution.py:100
  433.6 5.8 fusion.17
  443.9 6.1 fusion.2
  450.0 25.6 %reduce-scatter.19.cloned.1.call-done = f32[4,32,1152]{2,1,0:T(8,128)} async-done(((f32[4,128,1152]{2,1,0:T(8,128)}), f32[4,32,1152]{2,1,0:T(8,128)}) %reduce-scatter.19.cloned.1.call-update) | async-done | bytes 589840 | tf_op jit(solution)/shard_map/reduce_scatter | solution.py:58
  478.4 33.0 %reduce-scatter.17.cloned.1.call-done = f32[4,32,1152]{2,1,0:T(8,128)} async-done(((f32[4,128,1152]{2,1,0:T(8,128)}), f32[4,32,1152]{2,1,0:T(8,128)}) %reduce-scatter.17.cloned.1.call-update) | async-done | bytes 589840 | tf_op jit(solution)/shard_map/reduce_scatter | solution.py:58
  521.0 14.0 %collective-permute-done.5 = bf16[4,64,1152]{2,1,0:T(8,128)(2,1)S(1)} collective-permute-done((bf16[4,64,1152]{2,1,0:T(8,128)(2,1)S(1)}, bf16[4,64,1152]{2,1,0:T(8,128)(2,1)S(1)}, u32[]{:S(2)}, u32[]{:S(2)}) %collective-permute-start.5) | collective-permute-done | bytes 589856 | tf_op jit(solution)/shard_map/ppermute | solution.py:24
  543.7 34.7 %reduce-scatter.21.cloned.1.call-done = f32[4,32,1152]{2,1,0:T(8,128)} async-done(((f32[4,128,1152]{2,1,0:T(8,128)}), f32[4,32,1152]{2,1,0:T(8,128)}) %reduce-scatter.21.cloned.1.call-update) | async-done | bytes 589840 | tf_op jit(solution)/shard_map/reduce_scatter | solution.py:58
  598.5 5.7 convolution_bitcast_fusion.1
  609.6 8.6 copy.159
  618.2 9.0 reshape.214
  633.3 5.7 fusion.61
  639.9 11.0 gather_fusion.3
  658.2 8.4 gather_fusion.1
  678.8 78.5 %scatter_fusion = bf16[4,256,1152]{2,1,0:T(8,128)(2,1)} fusion(bf16[4,256,1152]{2,1,0:T(8,128)(2,1)} %broadcast_in_dim.28, s32[512]{0:T(512)S(1)} %get-tuple-element.153, bf16[512,1152]{1,0:T(8,128)(2,1)} %bitcast.188), kind=kCustom, calls=%fused_computation.4 | custom fusion | bytes 3543040 | tf_op jit(solution)/shard_map/scatter | solution.py:54
  757.2 78.7 %scatter_fusion.1 = bf16[4,256,1152]{2,1,0:T(8,128)(2,1)} fusion(bf16[4,256,1152]{2,1,0:T(8,128)(2,1)} %scatter_fusion, s32[512]{0:T(512)S(1)} %get-tuple-element.151, bf16[512,1152]{1,0:T(8,128)(2,1)} %bitcast.187), kind=kCustom, calls=%fused_computation.5 | custom fusion | bytes 3543040 | tf_op jit(solution)/shard_map/scatter | solution.py:54
  842.1 11.3 %psum.7 = f32[4,1152]{1,0:T(4,128)S(1)} all-reduce(f32[4,1152]{1,0:T(4,128)S(1)} %convolution_bitcast_fusion.5), channel_id=1, replica_groups=mesh['dp'=8,'mp'=4] {'mp'}, use_global_device_ids=true, to_apply=%region_26.30 | all-reduce | flops 4608 | bytes 36864 | tf_op jit(solution)/shard_map/psum | solution.py:242
  857.2 27.9 %reduce-scatter.33.cloned.1.call-done = f32[144,864]{1,0:T(8,128)} async-done(((f32[1152,864]{1,0:T(8,128)}), f32[144,864]{1,0:T(8,128)}) %reduce-scatter.33.cloned.1.call-update) | async-done | bytes 497680
  899.4 10.9 all-gather.14.cloned.1.call-done
  912.8 80.1 %scatter_fusion.2 = f32[4,256,1152]{2,1,0:T(8,128)} fusion(f32[4,256,1152]{2,1,0:T(8,128)} %broadcast_in_dim.35, s32[512]{0:T(512)S(1)} %get-tuple-element.153, f32[512,1152]{1,0:T(8,128)} %bitcast.197), kind=kCustom, calls=%fused_computation.6 | custom fusion | bytes 7081984 | tf_op jit(solution)/shard_map/scatter | solution.py:54
  992.9 79.7 %scatter_fusion.3 = f32[4,256,1152]{2,1,0:T(8,128)} fusion(f32[4,256,1152]{2,1,0:T(8,128)} %scatter_fusion.2, s32[512]{0:T(512)S(1)} %get-tuple-element.151, f32[512,1152]{1,0:T(8,128)} %bitcast.184), kind=kCustom, calls=%fused_computation.7 | custom fusion | bytes 7081984 | tf_op jit(solution)/shard_map/scatter | solution.py:54
  1072.6 21.2 %reduce-scatter.23.cloned.1.call-done = f32[144,6,288]{2,0,1:T(8,128)} async-done(((f32[1152,6,288]{2,0,1:T(8,128)}), f32[144,6,288]{2,0,1:T(8,128)}) %reduce-scatter.23.cloned.1.call-update) | async-done | bytes 995344 | tf_op jit(solution)/shard_map/reduce_scatter | solution.py:248
  (236 shorter events, 183.3 us)
Async XLA Ops:
  7.2 101.4 %all-gather.6.cloned.1.call-start = ((), (), s32[]{:S(2)}) async-start(), calls=%async_computation.10 | async-start | bytes 5971968 | tf_op jit(solution)/shard_map/all_gather | solution.py:96
  9.7 155.1 %all-gather.8.cloned.1.call-start = ((), (), s32[]{:S(2)}) async-start(), calls=%async_computation.11 | async-start | bytes 2985984 | tf_op jit(solution)/shard_map/all_gather | solution.py:97
  10.5 194.0 %reduce-scatter.15.cloned.1.call-start = ((), (), s32[]{:S(2)}) async-start(), calls=%async_computation.12 | async-start | bytes 2949120 | tf_op jit(solution)/shard_map/reduce_scatter | solution.py:58
  17.5 147.2 %copy-start.38 = (f32[4,128]{1,0:T(4,128)}, f32[4,128]{1,0:T(4,128)S(1)}, u32[]{:S(2)}) copy-start(f32[4,128]{1,0:T(4,128)S(1)} %broadcast_multiply_fusion.5) | copy-start | bytes 6148
  18.1 146.7 %copy-start.40 = (f32[4,128]{1,0:T(4,128)}, f32[4,128]{1,0:T(4,128)S(1)}, u32[]{:S(2)}) copy-start(f32[4,128]{1,0:T(4,128)S(1)} %add_rsqrt_fusion.1) | copy-start | bytes 6148
  172.8 89.7 %all-gather.10.cloned.1.call-start = ((), (), s32[]{:S(2)}) async-start(), calls=%async_computation.13 | async-start | bytes 2985984 | tf_op jit(solution)/shard_map/all_gather | solution.py:99
  174.8 200.4 %reduce-scatter.29.cloned.1.call-start = ((), (), s32[]{:S(2)}) async-start(), calls=%async_computation.22 | async-start | bytes 5971968 | tf_op jit(solution)/shard_map/reduce_scatter | solution.py:252
  207.8 15.2 %collective-permute-start = (bf16[4,32,1152]{2,1,0:T(8,128)(2,1)}, bf16[4,32,1152]{2,1,0:T(8,128)(2,1)}, u32[]{:S(2)}, u32[]{:S(2)}) collective-permute-start(bf16[4,32,1152]{2,1,0:T(8,128)(2,1)} %add_convert_fusion.2), channel_id=1, source_target_pairs={{0,3},{1,0},{2,1},{3,2},{4,7},{5,4},{6,5},{7,6},{8,11},{9,8},{10,9... | collective-permute-start | bytes 884744 | tf_op jit(solution)/shard_map/ppermute | solution.py:24
  224.9 16.1 %collective-permute-start.1 = (bf16[4,64,1152]{2,1,0:T(8,128)(2,1)}, bf16[4,64,1152]{2,1,0:T(8,128)(2,1)}, u32[]{:S(2)}, u32[]{:S(2)}) collective-permute-start(bf16[4,64,1152]{2,1,0:T(8,128)(2,1)} %pad_maximum_fusion.1), channel_id=1, source_target_pairs={{0,2},{1,3},{2,0},{3,1},{4,6},{5,7},{6,4},{7,5},{8,10},{9,11},{10,... | collective-permute-start | bytes 1769480 | tf_op jit(solution)/shard_map/ppermute | solution.py:24
  272.3 161.3 %all-gather.12.cloned.1.call-start = ((), (), s32[]{:S(2)}) async-start(), calls=%async_computation.14 | async-start | bytes 2985984 | tf_op jit(solution)/shard_map/all_gather | solution.py:100
  378.6 96.9 %reduce-scatter.19.cloned.1.call-start = ((), (), s32[]{:S(2)}) async-start(), calls=%async_computation.16 | async-start | bytes 2949120 | tf_op jit(solution)/shard_map/reduce_scatter | solution.py:58
  433.6 6.8 copy-start.47
  443.8 67.6 %reduce-scatter.17.cloned.1.call-start = ((), (), s32[]{:S(2)}) async-start(), calls=%async_computation.15 | async-start | bytes 2949120 | tf_op jit(solution)/shard_map/reduce_scatter | solution.py:58
  449.9 25.6 %copy-start.34 = (f32[4,32]{1,0:T(4,128)S(1)}, f32[4,32]{1,0:T(4,128)}, u32[]{:S(2)}) copy-start(f32[4,32]{1,0:T(4,128)} %copy-done.33) | copy-start | bytes 1540
  450.0 128.4 %reduce-scatter.21.cloned.1.call-start = ((), (), s32[]{:S(2)}) async-start(), calls=%async_computation.17 | async-start | bytes 2949120 | tf_op jit(solution)/shard_map/reduce_scatter | solution.py:58
  511.4 9.6 copy-start.37
  514.9 6.1 copy-start.7
  514.9 21.6 %copy-start.6 = (bf16[288,1152]{0,1:T(8,128)(2,1)S(1)}, bf16[288,1152]{0,1:T(8,128)(2,1)}, u32[]{:S(2)}) copy-start(bf16[288,1152]{0,1:T(8,128)(2,1)} %all_gather.29) | copy-start | bytes 1990660
  514.9 4.5 collective-permute-start.4
  519.4 15.5 %collective-permute-start.5 = (bf16[4,64,1152]{2,1,0:T(8,128)(2,1)S(1)}, bf16[4,64,1152]{2,1,0:T(8,128)(2,1)S(1)}, u32[]{:S(2)}, u32[]{:S(2)}) collective-permute-start(bf16[4,64,1152]{2,1,0:T(8,128)(2,1)S(1)} %pad_maximum_fusion.3), channel_id=1, source_target_pairs={{0,2},{1,3},{2,0},{3,1},{4,6},{5,7},{6,4},{7,5},{8,10},{9,11},{10,... | collective-permute-start | bytes 1769480 | tf_op jit(solution)/shard_map/ppermute | solution.py:24
  521.0 16.1 %copy-start.2 = (f32[4,4,128,128]{2,3,1,0:T(8,128)S(1)}, f32[4,4,128,128]{2,3,1,0:T(8,128)}, u32[]{:S(2)}) copy-start(f32[4,4,128,128]{2,3,1,0:T(8,128)} %copy-done.1) | copy-start | bytes 3145732
  521.0 16.1 %copy-start.21 = (bf16[1,4,128,288]{2,3,0,1:T(8,128)(2,1)S(1)}, bf16[1,4,128,288]{2,3,0,1:T(8,128)(2,1)}, u32[]{:S(2)}) copy-start(bf16[1,4,128,288]{2,3,0,1:T(8,128)(2,1)} %copy-done.20) | copy-start | bytes 884740
  543.6 88.0 %reduce-scatter.31.cloned.1.call-start = ((), (), s32[]{:S(2)}) async-start(), calls=%async_computation.23 | async-start | bytes 737280
  595.0 241.0 %reduce-scatter.25.cloned.1.call-start = ((), (), s32[]{:S(2)}) async-start(), calls=%async_computation.20 | async-start | bytes 1990656 | tf_op jit(solution)/shard_map/reduce_scatter | solution.py:250
  598.5 255.6 %reduce-scatter.27.cloned.1.call-start = ((), (), s32[]{:S(2)}) async-start(), calls=%async_computation.21 | async-start | bytes 5971968 | tf_op jit(solution)/shard_map/reduce_scatter | solution.py:251
  604.2 280.8 %reduce-scatter.33.cloned.1.call-start = ((), (), s32[]{:S(2)}) async-start(), calls=%async_computation.24 | async-start | bytes 4644864
  627.2 6.1 copy-start.30
  627.2 283.1 %all-gather.14.cloned.1.call-start = ((), (), s32[]{:S(2)}) async-start(), calls=%async_computation.18 | async-start | bytes 2949120 | tf_op jit(solution)/shard_map/all_gather | solution.py:227
  631.6 462.2 %reduce-scatter.23.cloned.1.call-start = ((), (), s32[]{:S(2)}) async-start(), calls=%async_computation.19 | async-start | bytes 11943936 | tf_op jit(solution)/shard_map/reduce_scatter | solution.py:248
  639.9 11.0 collective-permute-start.2
  651.8 21.9 %collective-permute-start.3 = (bf16[4,64,1152]{2,1,0:T(8,128)(2,1)}, bf16[4,64,1152]{2,1,0:T(8,128)(2,1)}, u32[]{:S(2)}, u32[]{:S(2)}) collective-permute-start(bf16[4,64,1152]{2,1,0:T(8,128)(2,1)} %pad_maximum_fusion.2), channel_id=1, source_target_pairs={{0,2},{1,3},{2,0},{3,1},{4,6},{5,7},{6,4},{7,5},{8,10},{9,11},{10,... | collective-permute-start | bytes 1769480 | tf_op jit(solution)/shard_map/ppermute | solution.py:24
  757.2 78.7 %copy-start.23 = (f32[288,144]{0,1:T(8,128)S(1)}, f32[288,144]{0,1:T(8,128)}, u32[]{:S(2)}) copy-start(f32[288,144]{0,1:T(8,128)} %param.35) | copy-start | bytes 497668
  (39 other events, 71.4 us)
Sparse Core Ops, SparseCore 0:
  10.9 97.7 all-gather.5
  111.5 53.2 all-gather.7
  172.9 31.5 reduce-scatter.14
  207.4 55.0 all-gather.9
  272.4 102.7 reduce-scatter.28
  378.8 54.7 all-gather.11
  443.9 31.6 reduce-scatter.18
  478.3 33.0 reduce-scatter.16
  543.7 34.5 reduce-scatter.20
  595.1 22.0 reduce-scatter.30
  621.1 66.1 reduce-scatter.24
  690.7 102.8 reduce-scatter.26
  797.6 87.3 reduce-scatter.32
  886.5 23.8 all-gather.13
  913.8 179.9 reduce-scatter.22
